TPU v7x, 32 devices: a whole 2x2x4 slice. The times are simulated.
32 devices in a mesh: pair: 2 (over x), blk: 8 (over z, y), group: 2 (over core).
Axes of the slice: x: 2, y: 2, z: 4, core: 2. Of those that a mesh axis runs over, the one named last changes fastest.
Arguments:
- codes: int32 [32, 1536, 256], P(('pair', 'blk', 'group')), may hold values from 0 to 255
- scales: int32 [32, 1536, 8], P(('pair', 'blk', 'group')), may hold values from -7 to 0
- inputs: bfloat16 [4096, 1536], P(('pair', 'blk', 'group')), may hold values from -6 to 6
- cotangent: bfloat16 [4096, 256], P(('pair', 'blk', 'group')), may hold values from -6 to 6
Outputs:
- earlier_grad: float32 [1536, 256], replicated
- current_grad: float32 [1536, 256], replicated
All inputs are finite; a program needn't handle non-finite values.
Results may differ from a plain program's by a relative error of at most 0.0003.
Values sent between devices are 32-bit elements; how exact they have to be, the bound alone decides.
No kernel may reach another device: no remote copies, remote signals or barrier semaphores. Data moves between devices by JAX's collectives and lax.ppermute only.
A program may use at most 64 MiB of HBM per device.

v0:
```python
import jax
import jax.numpy as jnp
from jax import lax
from jax.sharding import PartitionSpec as P


def decode(codes, scales):
    codes = codes[0]
    scales = scales[0]
    rows, width = codes.shape
    sign = 1.0 - 2.0 * (codes // 128).astype(jnp.float32)
    field = codes // 8 % 16
    mant = (codes % 8).astype(jnp.float32)
    frac = jnp.where(field > 0, 8.0 + mant, mant)
    power = jnp.where(field > 0, field, 1) - 10
    expo = power.reshape(rows, scales.shape[1], width // scales.shape[1]) + scales[:, :, None]
    return sign * frac * jnp.exp2(expo.reshape(rows, width).astype(jnp.float32))


def combine(stack, count):
    pooled = lax.psum(stack, "pair")
    share = lax.psum_scatter(pooled, "blk", scatter_dimension=1, tiled=True)
    total = lax.psum_scatter(share, "group", scatter_dimension=1, tiled=True) / count
    return lax.all_gather(total, ("blk", "group"), axis=1, tiled=True)


def key_product(inputs, cotangent):
    return lax.dot_general(
        inputs, cotangent, (((0,), (0,)), ((), ())), preferred_element_type=jnp.float32
    )


def local(codes, scales, inputs, cotangent):
    count = lax.axis_size("pair") * lax.axis_size("blk") * lax.axis_size("group")
    decoded = decode(codes, scales)
    product = key_product(inputs, cotangent)
    summed = combine(jnp.stack([decoded, product]), count)
    earlier_grad = summed[0]
    current_grad = summed[1]
    return (earlier_grad, current_grad)


def solution(mesh):
    in_specs = (
        P(("pair", "blk", "group"), None, None),
        P(("pair", "blk", "group"), None, None),
        P(("pair", "blk", "group"), None),
        P(("pair", "blk", "group"), None),
    )
    out_specs = (P(), P())
    return jax.shard_map(local, mesh=mesh, in_specs=in_specs, out_specs=out_specs, check_vma=False)
```

profile of v0, /device:TPU:0, one launch (start us, length us, event | category | flops | bytes accessed | tf_op | source)
XLA Modules:
  0.0 186.2 jit_solution(1373778970033017761)
XLA Ops:
  7.2 0.0 copy-start
  7.2 0.0 reduce-scatter.3.cloned.1.call-start
  7.2 1.0 add.58
  8.2 0.5 copy.7
  8.7 0.0 copy-start.1
  8.7 4.5 %fusion.5 = f32[1,1536,256]{2,1,0:T(8,128)S(1)} fusion(s32[1,1536,256]{2,1,0:T(8,128)S(1)} %copy.7, s32[1,1536,256]{2,1,0:T(8,128)} %param.4), kind=kLoop, calls=%fused_computation.20 | loop fusion | flops 21233664 | bytes 4718592 | tf_op jit(solution)/shard_map/mul | solution.py:17
  13.2 0.0 copy-done
  13.2 0.0 copy-done.1
  13.3 0.4 convolution_bitcast_fusion
  13.6 1.9 pad_maximum_fusion
  15.5 0.0 reduce-scatter.3.cloned.1.call-update
  15.5 0.0 reduce-scatter.5.cloned.1.call-start
  15.6 77.1 %reduce-scatter.3.cloned.1.call-done = f32[2,192,256]{2,1,0:T(8,128)} async-done(((f32[2,1536,256]{2,1,0:T(8,128)}), f32[2,192,256]{2,1,0:T(8,128)}) %reduce-scatter.3.cloned.1.call-update) | async-done | bytes 393232 | tf_op jit(solution)/shard_map/reduce_scatter | solution.py:22
  92.7 0.0 reduce-scatter.5.cloned.1.call-update
  92.7 0.0 all-reduce.2.cloned.1.call-start
  92.8 9.1 %reduce-scatter.5.cloned.1.call-done = f32[2,96,256]{2,1,0:T(8,128)} async-done(((f32[2,192,256]{2,1,0:T(8,128)}), f32[2,96,256]{2,1,0:T(8,128)}) %reduce-scatter.5.cloned.1.call-update) | async-done | bytes 196624 | tf_op jit(solution)/shard_map/reduce_scatter | solution.py:23
  101.9 0.0 all-reduce.2.cloned.1.call-update
  101.9 0.0 all-gather.2.cloned.1.call-start
  102.0 25.8 %all-reduce.2.cloned.1.call-done = f32[2,96,256]{2,1,0:T(8,128)} async-done(((f32[2,96,256]{2,1,0:T(8,128)}), f32[2,96,256]{2,1,0:T(8,128)}) %all-reduce.2.cloned.1.call-update) | async-done | bytes 196624 | tf_op jit(solution)/shard_map/psum | solution.py:21
  127.7 1.6 broadcast_multiply_fusion
  129.3 0.0 all-gather.2.cloned.1.call-update
  129.4 46.6 %all-gather.2.cloned.1.call-done = f32[2,1536,256]{2,1,0:T(8,128)} async-done(((f32[2,96,256]{2,1,0:T(8,128)}), f32[2,1536,256]{2,1,0:T(8,128)}) %all-gather.2.cloned.1.call-update) | async-done | bytes 3145744 | tf_op jit(solution)/shard_map/all_gather | solution.py:24
  176.0 3.7 %slice_bitcast_fusion = (f32[1536,256]{1,0:T(8,128)}, f32[1536,256]{1,0:T(8,128)}) fusion(f32[2,1536,256]{2,1,0:T(8,128)} %all-gather.2.cloned.1.call-done), kind=kLoop, calls=%fused_computation.28 | loop fusion | bytes 6291456 | tf_op jit(solution)/shard_map/squeeze | solution.py:39
Async XLA Ops:
  7.2 6.1 %copy-start = (bf16[128,1536]{1,0:T(8,128)(2,1)S(1)}, bf16[128,1536]{1,0:T(8,128)(2,1)}, u32[]{:S(2)}) copy-start(bf16[128,1536]{1,0:T(8,128)(2,1)} %param.6) | copy-start | bytes 1179652
  7.2 85.5 %reduce-scatter.3.cloned.1.call-start = ((), (), s32[]{:S(2)}) async-start(), calls=%async_computation.3 | async-start | bytes 3538944 | tf_op jit(solution)/shard_map/reduce_scatter | solution.py:22
  8.7 4.5 %copy-start.1 = (bf16[128,256]{1,0:T(8,128)(2,1)S(1)}, bf16[128,256]{1,0:T(8,128)(2,1)}, u32[]{:S(2)}) copy-start(bf16[128,256]{1,0:T(8,128)(2,1)} %param.7) | copy-start | bytes 196612
  15.5 86.4 %reduce-scatter.5.cloned.1.call-start = ((), (), s32[]{:S(2)}) async-start(), calls=%async_computation.4 | async-start | bytes 589824 | tf_op jit(solution)/shard_map/reduce_scatter | solution.py:23
  92.7 35.0 %all-reduce.2.cloned.1.call-start = ((), (), s32[]{:S(2)}) async-start(), calls=%async_computation.5 | async-start | bytes 393216 | tf_op jit(solution)/shard_map/psum | solution.py:21
  101.9 74.0 %all-gather.2.cloned.1.call-start = ((), (), s32[]{:S(2)}) async-start(), calls=%async_computation.2 | async-start | bytes 3342336 | tf_op jit(solution)/shard_map/all_gather | solution.py:24
Sparse Core Ops, SparseCore 0:
  15.7 77.0 reduce-scatter.2
  94.9 6.8 reduce-scatter.4
  104.2 23.5 all-reduce.1
  130.4 45.4 all-gather.1
where the time goes:
time: 186 us
  waiting for transfers between devices  159 us (85%)
  between operations  13.8 us (7%)
  other arithmetic  7.97 us (4%)
  local copies, waits for them, and re-layouts  5.23 us (3%)
    reduce_scatter x1, waiting for transfers between devices, combine(): share = lax.psum_scatter(pooled, 'blk', scatter_dimension=1, tiled=True)  77.1 us
    all_gather x1, waiting for transfers between devices, combine(): return lax.all_gather(total, ('blk', 'group'), axis=1, tiled=True)  46.6 us
    psum x1, waiting for transfers between devices, combine(): pooled = lax.psum(stack, 'pair')  25.8 us
    reduce_scatter x1, waiting for transfers between devices, combine(): lax.psum_scatter(share, 'group', scatter_dimension=1, tiled=True) / count  9.11 us
    mul x1, other arithmetic, decode(): return sign * frac * jnp.exp2(expo.reshape(rows, width).astype(jnp.float32))  4.5 us
    squeeze x1, local copies, waits for them, and re-layouts, local(): current_grad = summed[1]  3.74 us
  transfers between devices with their start and end apart: 4, of which 4 were waited for; matrix products, arithmetic and copies ran while one was open for 0% of the time, Pallas kernels for 0%

commit v1 on v0

--- a/solution.py
+++ b/solution.py
@@ -21,7 +21,7 @@
     pooled = lax.psum(stack, "pair")
     share = lax.psum_scatter(pooled, "blk", scatter_dimension=1, tiled=True)
     total = lax.psum_scatter(share, "group", scatter_dimension=1, tiled=True) / count
-    return lax.all_gather(total, ("blk", "group"), axis=1, tiled=True)
+    return jnp.concatenate(lax.all_gather(total, ("blk", "group")), axis=1)
 
 
 def key_product(inputs, cotangent):

time: 186 us -> 187 us (level)
    slice x0 -> x1, local copies, waits for them, and re-layouts: none -> 3.87 us  [local(): current_grad = summed[1]]
    squeeze x1 -> x0, local copies, waits for them, and re-layouts: 3.74 us -> none  [local(): current_grad = summed[1]]
where the time goes in v1:
time: 187 us; the launch traced here: 186 us
  waiting for transfers between devices  159 us (85%)
  between operations  13.8 us (7%)
  other arithmetic  7.97 us (4%)
  local copies, waits for them, and re-layouts  5.36 us (3%)
    reduce_scatter x1, waiting for transfers between devices, combine(): share = lax.psum_scatter(pooled, 'blk', scatter_dimension=1, tiled=True)  77.1 us
    all_gather x1, waiting for transfers between devices, combine(): return jnp.concatenate(lax.all_gather(total, ('blk', 'group')), axis=1)  46.5 us
    psum x1, waiting for transfers between devices, combine(): pooled = lax.psum(stack, 'pair')  25.8 us
    reduce_scatter x1, waiting for transfers between devices, combine(): lax.psum_scatter(share, 'group', scatter_dimension=1, tiled=True) / count  9.11 us
    mul x1, other arithmetic, decode(): return sign * frac * jnp.exp2(expo.reshape(rows, width).astype(jnp.float32))  4.5 us
    slice x1, local copies, waits for them, and re-layouts, local(): current_grad = summed[1]  3.87 us
  transfers between devices with their start and end apart: 4, of which 4 were waited for; matrix products, arithmetic and copies ran while one was open for 0% of the time, Pallas kernels for 0%

profile of v1, /device:TPU:0, one launch (start us, length us, event | category | flops | bytes accessed | tf_op | source)
XLA Modules:
  0.0 186.3 jit_solution(7870009971666345618)
XLA Ops:
  7.2 0.0 copy-start
  7.2 0.0 reduce-scatter.3.cloned.1.call-start
  7.2 1.0 add.58
  8.2 0.5 copy.8
  8.7 0.0 copy-start.1
  8.7 4.5 %fusion.5 = f32[1,1536,256]{2,1,0:T(8,128)S(1)} fusion(s32[1,1536,256]{2,1,0:T(8,128)S(1)} %copy.8, s32[1,1536,256]{2,1,0:T(8,128)} %param.4), kind=kLoop, calls=%fused_computation.20 | loop fusion | flops 21233664 | bytes 4718592 | tf_op jit(solution)/shard_map/mul | solution.py:17
  13.2 0.0 copy-done
  13.2 0.0 copy-done.1
  13.3 0.4 convolution_bitcast_fusion
  13.6 1.9 pad_maximum_fusion
  15.5 0.0 reduce-scatter.3.cloned.1.call-update
  15.5 0.0 reduce-scatter.5.cloned.1.call-start
  15.6 77.1 %reduce-scatter.3.cloned.1.call-done = f32[2,192,256]{2,1,0:T(8,128)} async-done(((f32[2,1536,256]{2,1,0:T(8,128)}), f32[2,192,256]{2,1,0:T(8,128)}) %reduce-scatter.3.cloned.1.call-update) | async-done | bytes 393232 | tf_op jit(solution)/shard_map/reduce_scatter | solution.py:22
  92.7 0.0 reduce-scatter.5.cloned.1.call-update
  92.7 0.0 all-reduce.2.cloned.1.call-start
  92.8 9.1 %reduce-scatter.5.cloned.1.call-done = f32[2,96,256]{2,1,0:T(8,128)} async-done(((f32[2,192,256]{2,1,0:T(8,128)}), f32[2,96,256]{2,1,0:T(8,128)}) %reduce-scatter.5.cloned.1.call-update) | async-done | bytes 196624 | tf_op jit(solution)/shard_map/reduce_scatter | solution.py:23
  101.9 0.0 all-reduce.2.cloned.1.call-update
  101.9 0.0 all-gather.3.cloned.1.call-start
  102.0 25.8 %all-reduce.2.cloned.1.call-done = f32[2,96,256]{2,1,0:T(8,128)} async-done(((f32[2,96,256]{2,1,0:T(8,128)}), f32[2,96,256]{2,1,0:T(8,128)}) %all-reduce.2.cloned.1.call-update) | async-done | bytes 196624 | tf_op jit(solution)/shard_map/psum | solution.py:21
  127.7 1.6 broadcast_multiply_fusion
  129.3 0.0 all-gather.3.cloned.1.call-update
  129.4 46.5 %all-gather.3.cloned.1.call-done = f32[32,96,256]{2,1,0:T(8,128)} async-done(((f32[2,96,256]{2,1,0:T(8,128)}), f32[32,96,256]{2,1,0:T(8,128)}) %all-gather.3.cloned.1.call-update) | async-done | bytes 3145744 | tf_op jit(solution)/shard_map/all_gather | solution.py:24
  175.9 3.9 %fusion.15 = (f32[1,16,96,256]{3,2,0,1:T(8,128)}, f32[1,16,96,256]{3,2,0,1:T(8,128)}) fusion(f32[2,16,96,256]{3,2,0,1:T(8,128)} %bitcast.12), kind=kLoop, calls=%fused_computation.32 | loop fusion | bytes 6291456 | tf_op jit(solution)/shard_map/slice | solution.py:39
Async XLA Ops:
  7.2 6.1 %copy-start = (bf16[128,1536]{1,0:T(8,128)(2,1)S(1)}, bf16[128,1536]{1,0:T(8,128)(2,1)}, u32[]{:S(2)}) copy-start(bf16[128,1536]{1,0:T(8,128)(2,1)} %param.6) | copy-start | bytes 1179652
  7.2 85.5 %reduce-scatter.3.cloned.1.call-start = ((), (), s32[]{:S(2)}) async-start(), calls=%async_computation.3 | async-start | bytes 3538944 | tf_op jit(solution)/shard_map/reduce_scatter | solution.py:22
  8.7 4.5 %copy-start.1 = (bf16[128,256]{1,0:T(8,128)(2,1)S(1)}, bf16[128,256]{1,0:T(8,128)(2,1)}, u32[]{:S(2)}) copy-start(bf16[128,256]{1,0:T(8,128)(2,1)} %param.7) | copy-start | bytes 196612
  15.5 86.4 %reduce-scatter.5.cloned.1.call-start = ((), (), s32[]{:S(2)}) async-start(), calls=%async_computation.4 | async-start | bytes 589824 | tf_op jit(solution)/shard_map/reduce_scatter | solution.py:23
  92.7 35.0 %all-reduce.2.cloned.1.call-start = ((), (), s32[]{:S(2)}) async-start(), calls=%async_computation.5 | async-start | bytes 393216 | tf_op jit(solution)/shard_map/psum | solution.py:21
  101.9 74.0 %all-gather.3.cloned.1.call-start = ((), (), s32[]{:S(2)}) async-start(), calls=%async_computation.2 | async-start | bytes 3342336 | tf_op jit(solution)/shard_map/all_gather | solution.py:24
Sparse Core Ops, SparseCore 0:
  15.7 77.0 reduce-scatter.2
  94.9 6.8 reduce-scatter.4
  104.2 23.5 all-reduce.1
  130.4 45.4 all-gather.2
